TPU v7x, 512 devices: a whole 4x8x8 slice. The times are simulated.
512 devices in a mesh: space: 64 (over y, x, z_hi), chan: 8 (over z_lo, core).
Axes of the slice: x: 4, y: 8, z: 8 (z_hi: 2, z_lo: 4; z = z_hi * 4 + z_lo), core: 2. Of those that a mesh axis runs over, the one named last changes fastest.
Arguments:
- source: bfloat16 [512, 192, 128], P('chan', 'space'), may hold values from -6 to 6
- kernel: bfloat16 [7, 7, 512, 512], P(None, None, 'chan'), may hold values from -0.0390625 to 0.0390625
Outputs:
- image: bfloat16 [512, 192, 128], P('chan', 'space')
All inputs are finite; a program needn't handle non-finite values.
Results may differ from a plain program's by a relative error of at most 0.001.
Values may be sent and summed in bfloat16 or wider, within the bound.
A program may use at most 64 MiB of HBM per device.

v0:
```python
import jax
import jax.numpy as jnp
from jax import lax
from jax.sharding import PartitionSpec as P

OFF = 7


def padded_2(array, sides, width):
    for axis, dim in sides:
        devices, length = (lax.axis_size(axis), array.shape[dim])
        up = [(i, (i + 1) % devices) for i in range(devices - 1)]
        down = [(j, i) for i, j in up]
        last = lax.slice_in_dim(array, length - width, length, axis=dim)
        initial = lax.slice_in_dim(array, 0, width, axis=dim)
        before = lax.ppermute(last, axis, up)
        after = lax.ppermute(initial, axis, down)
        array = jnp.concatenate([before, array, after], axis=dim)
    return array


def correlate(kernel, padded, height):
    reach = (OFF - 1) // 2
    width_cols = padded.shape[2]
    widened = jnp.pad(padded, ((0, 0), (0, 0), (reach, reach)))
    total = jnp.zeros((kernel.shape[2], height, width_cols), jnp.float32)
    for row_shift in range(OFF):
        window = widened[:, row_shift : row_shift + height, :]
        stacked = jnp.stack(
            [window[:, :, col_shift : col_shift + width_cols] for col_shift in range(OFF)]
        )
        weights = kernel[row_shift]
        total = total + jnp.einsum(
            "boc,bcxy->oxy", weights, stacked, preferred_element_type=jnp.float32
        )
    return total


def shards(source, kernel):
    reach = (OFF - 1) // 2
    height = source.shape[1]
    rimmed = padded_2(source, (("space", 1),), reach)
    coupled = correlate(kernel, lax.all_gather(rimmed, "chan", axis=0, tiled=True), height)
    return (source.astype(jnp.float32) - coupled).astype(jnp.bfloat16)


def solution(mesh):
    placed = (P("chan", "space", None), P(None, None, "chan", None))
    return jax.shard_map(
        shards, mesh=mesh, in_specs=placed, out_specs=P("chan", "space", None), check_vma=False
    )
```

profile of v0, /device:TPU:2, one launch (start us, length us, event | category | flops | bytes accessed | tf_op | source)
XLA Modules:
  0.0 92.9 jit_solution(15703168403566414398)
XLA Ops:
  6.5 10.9 %collective-permute-start = (bf16[64,3,128]{2,0,1:T(8,128)(2,1)}, bf16[64,3,128]{2,0,1:T(8,128)(2,1)S(1)}, u32[]{:S(2)}, u32[]{:S(2)}) collective-permute-start(bf16[64,3,128]{2,0,1:T(8,128)(2,1)} %param.2), channel_id=1, source_target_pairs={{0,8},{8,16},{16,24},{24,32},{32,40},{40,48},{48,56},{56,64},{64,7... | collective-permute-start | bytes 147464 | tf_op jit(solution)/shard_map/ppermute | solution.py:16
  17.5 1.9 %collective-permute-start.1 = (bf16[64,3,128]{2,0,1:T(8,128)(2,1)}, bf16[64,3,128]{2,0,1:T(8,128)(2,1)S(1)}, u32[]{:S(2)}, u32[]{:S(2)}) collective-permute-start(bf16[64,3,128]{2,0,1:T(8,128)(2,1)} %param.2), channel_id=1, source_target_pairs={{8,0},{16,8},{24,16},{32,24},{40,32},{48,40},{56,48},{64,56},{72,6... | collective-permute-start | bytes 147464 | tf_op jit(solution)/shard_map/ppermute | solution.py:17
  19.4 1.1 %collective-permute-done = bf16[64,3,128]{2,0,1:T(8,128)(2,1)S(1)} collective-permute-done((bf16[64,3,128]{2,0,1:T(8,128)(2,1)}, bf16[64,3,128]{2,0,1:T(8,128)(2,1)S(1)}, u32[]{:S(2)}, u32[]{:S(2)}) %collective-permute-start) | collective-permute-done | bytes 49184 | tf_op jit(solution)/shard_map/ppermute | solution.py:16
  20.5 7.9 %collective-permute-done.1 = bf16[64,3,128]{2,0,1:T(8,128)(2,1)S(1)} collective-permute-done((bf16[64,3,128]{2,0,1:T(8,128)(2,1)}, bf16[64,3,128]{2,0,1:T(8,128)(2,1)S(1)}, u32[]{:S(2)}, u32[]{:S(2)}) %collective-permute-start.1) | collective-permute-done | bytes 49184 | tf_op jit(solution)/shard_map/ppermute | solution.py:17
  28.4 1.5 %pad_maximum_fusion = bf16[64,9,128]{2,0,1:T(8,128)(2,1)} fusion(bf16[64,3,128]{2,0,1:T(8,128)(2,1)S(1)} %collective-permute-done.1, bf16[64,3,128]{2,0,1:T(8,128)(2,1)} %param.2, bf16[64,3,128]{2,0,1:T(8,128)(2,1)S(1)} %collective-permute-done), kind=kLoop, calls=%fused_computation.170 | loop fusion | flops 147456 | bytes 294912 | tf_op jit(solution)/shard_map/concatenate | solution.py:18
  29.9 39.3 %all-gather.2.cloned.1.call-done = bf16[512,9,128]{2,0,1:T(8,128)(2,1)} async-done(((bf16[64,9,128]{2,0,1:T(8,128)(2,1)}), bf16[512,9,128]{2,0,1:T(8,128)(2,1)}) %all-gather.2.cloned.1.call-update) | async-done | bytes 1179664 | tf_op jit(solution)/shard_map/all_gather | solution.py:43
  69.2 1.3 %fusion.36 = bf16[7,512,3,128]{3,1,2,0:T(8,128)(2,1)S(1)} fusion(bf16[512,9,128]{2,0,1:T(8,128)(2,1)} %all-gather.2.cloned.1.call-done), kind=kLoop, calls=%fused_computation.85 | loop fusion | bytes 1572864
  70.5 1.2 %fusion.38 = bf16[7,512,3,128]{3,1,2,0:T(8,128)(2,1)S(1)} fusion(bf16[7,512,3,128]{3,1,2,0:T(8,128)(2,1)S(1)} %fusion.36, bf16[512,9,128]{2,0,1:T(8,128)(2,1)} %all-gather.2.cloned.1.call-done), kind=kLoop, calls=%fused_computation.87 | loop fusion | bytes 1572864
  71.7 0.2 fusion.40
  72.0 0.2 fusion.42
  72.2 0.2 fusion.44
  72.5 0.8 fusion.46
  73.3 0.2 fusion.50
  73.5 0.2 fusion.52
  73.8 0.2 fusion.54
  74.0 0.2 fusion.56
  74.3 1.0 %fusion.58 = (bf16[7,512,3,128]{3,1,2,0:T(8,128)(2,1)S(1)}, bf16[7,512,3,128]{3,1,2,0:T(8,128)(2,1)S(1)}, bf16[7,512,3,128]{3,1,2,0:T(8,128)(2,1)S(1)}, bf16[7,5...) fusion(bf16[7,512,3,128]{3,1,2,0:T(8,128)(2,1)S(1)} %fusion.56, bf16[512,9,128]{2,0,1:T(8,128)(2,1)S(1)} %copy-done, ...), kind=kLoop, calls=%fused_computation.107 | loop fusion | bytes 3145728 | tf_op jit(solution)/shard_map/stack | solution.py:29
  75.3 0.2 fusion.64
  75.5 0.2 fusion.66
  75.8 0.2 fusion.68
  76.0 0.8 fusion.70
  77.1 0.4 fusion.80
  77.5 0.6 fusion.82
  78.3 0.4 fusion.94
  79.0 1.0 %copy-done.1 = bf16[7,7,64,512]{3,2,1,0:T(8,128)(2,1)S(1)} copy-done((bf16[7,7,64,512]{3,2,1,0:T(8,128)(2,1)S(1)}, bf16[7,7,64,512]{3,2,1,0:T(8,128)(2,1)}, u32[]{:S(2)}) %copy-start.1) | copy-done | bytes 3211288
  80.0 0.6 convolution_bitcast_fusion
  80.6 0.6 convolution_bitcast_fusion.1
  81.1 0.6 convolution_bitcast_fusion.2
  81.7 0.6 convolution_bitcast_fusion.3
  82.3 0.6 convolution_bitcast_fusion.4
  82.8 0.6 convolution_bitcast_fusion.5
  84.8 1.2 %fusion.8 = bf16[64,3,128]{2,0,1:T(8,128)(2,1)} fusion(f32[3,128,64]{1,2,0:T(8,128)S(1)} %convolution_bitcast_fusion, f32[3,128,64]{1,2,0:T(8,128)S(1)} %convolution_bitcast_fusion.1, f32[3,128,64]{1,2,0:T(8,128)S(1)} %convolution_bitcast_fusion.2, f32[3,128,64]{1,2,0:T(8,128)S(1)} %convolution_bitcast_fusion.3, ...), kind=kOutput, calls=%fused_computation.57 | convolution fusion | flops 176381952 | bytes 3899392 | tf_op jit(solution)/shard_map/boc,bcxy->oxy/dot_general | solution.py:33
  (21 shorter events, 2.3 us)
Async XLA Ops:
  6.5 62.7 %all-gather.2.cloned.1.call-start = ((), (), s32[]{:S(2)}) async-start(), calls=%async_computation | async-start | bytes 1327104 | tf_op jit(solution)/shard_map/all_gather | solution.py:43
  6.5 13.9 %collective-permute-start = (bf16[64,3,128]{2,0,1:T(8,128)(2,1)}, bf16[64,3,128]{2,0,1:T(8,128)(2,1)S(1)}, u32[]{:S(2)}, u32[]{:S(2)}) collective-permute-start(bf16[64,3,128]{2,0,1:T(8,128)(2,1)} %param.2), channel_id=1, source_target_pairs={{0,8},{8,16},{16,24},{24,32},{32,40},{40,48},{48,56},{56,64},{64,7... | collective-permute-start | bytes 147464 | tf_op jit(solution)/shard_map/ppermute | solution.py:16
  17.5 11.0 %collective-permute-start.1 = (bf16[64,3,128]{2,0,1:T(8,128)(2,1)}, bf16[64,3,128]{2,0,1:T(8,128)(2,1)S(1)}, u32[]{:S(2)}, u32[]{:S(2)}) collective-permute-start(bf16[64,3,128]{2,0,1:T(8,128)(2,1)} %param.2), channel_id=1, source_target_pairs={{8,0},{16,8},{24,16},{32,24},{40,32},{48,40},{56,48},{64,56},{72,6... | collective-permute-start | bytes 147464 | tf_op jit(solution)/shard_map/ppermute | solution.py:17
  69.2 2.5 %copy-start = (bf16[512,9,128]{2,0,1:T(8,128)(2,1)S(1)}, bf16[512,9,128]{2,0,1:T(8,128)(2,1)}, u32[]{:S(2)}) copy-start(bf16[512,9,128]{2,0,1:T(8,128)(2,1)} %all-gather.2.cloned.1.call-done) | copy-start | bytes 3538948
  78.1 1.9 %copy-start.1 = (bf16[7,7,64,512]{3,2,1,0:T(8,128)(2,1)S(1)}, bf16[7,7,64,512]{3,2,1,0:T(8,128)(2,1)}, u32[]{:S(2)}) copy-start(bf16[7,7,64,512]{3,2,1,0:T(8,128)(2,1)} %param.3) | copy-start | bytes 9633796
  84.0 0.8 copy-start.2
Sparse Core Ops, SparseCore 0:
  30.0 39.1 all-gather.1
where the time goes:
time: 93.2 us; the launch traced here: 92.9 us
  waiting for transfers between devices  48.3 us (52%)
  between operations  13.6 us (15%)
  starting transfers between devices  12.8 us (14%)
  local copies, waits for them, and re-layouts  12 us (13%)
  matrix products  4.56 us (5%)
  other arithmetic  1.48 us (2%)
    all_gather x1, waiting for transfers between devices, shards(): lax.all_gather(rimmed, 'chan', axis=0, tiled=True)  39.3 us
    ppermute x1, starting transfers between devices, padded_2(): before = lax.ppermute(last, axis, up)  10.9 us
    unnamed x31, local copies, waits for them, and re-layouts  7.99 us
    ppermute x1, waiting for transfers between devices, padded_2(): after = lax.ppermute(initial, axis, down)  7.92 us
    dot_general x7, matrix products, correlate(): jnp.einsum('boc,bcxy->oxy', weights, stacked, preferred_element_type=jnp....  4.56 us
    another operation x7, local copies, waits for them, and re-layouts, correlate(): jnp.stack([window[:, :, col_shift:col_shift + width_cols] for col_shift i...  4.06 us
    ppermute x1, starting transfers between devices, padded_2(): after = lax.ppermute(initial, axis, down)  1.92 us
  transfers between devices with their start and end apart: 3, of which 3 were waited for; matrix products, arithmetic and copies ran while one was open for 0% of the time, Pallas kernels for 0%

commit v1 on v0

--- a/solution.py
+++ b/solution.py
@@ -2,6 +2,7 @@
 import jax.numpy as jnp
 from jax import lax
 from jax.sharding import PartitionSpec as P
+from jax.lax import all_to_all, axis_size
 
 OFF = 7
 
@@ -40,7 +41,14 @@
     reach = (OFF - 1) // 2
     height = source.shape[1]
     rimmed = padded_2(source, (("space", 1),), reach)
-    coupled = correlate(kernel, lax.all_gather(rimmed, "chan", axis=0, tiled=True), height)
+    coupled = correlate(
+        kernel,
+        jnp.concatenate(
+            all_to_all(jnp.stack([rimmed for _ in range(axis_size("chan"))], axis=0), "chan", 0, 0),
+            axis=0,
+        ),
+        height,
+    )
     return (source.astype(jnp.float32) - coupled).astype(jnp.bfloat16)
 
 

time: 93.2 us -> 71.8 us (0.77)
  the two profiles are of different devices: /device:TPU:2 before, /device:TPU:1 now
where the time goes in v1:
time: 71.8 us; the launch traced here: 71.5 us
  blocking collectives  35.1 us (49%)
  starting transfers between devices  12.7 us (18%)
  local copies, waits for them, and re-layouts  10.3 us (14%)
  waiting for transfers between devices  7.71 us (11%)
  matrix products  4.57 us (6%)
  other arithmetic  0.82 us (1%)
    all_to_all x1, blocking collectives, shards(): all_to_all(jnp.stack([rimmed for _ in range(axis_size('chan'))], axis=0),...  35.1 us
    ppermute x1, starting transfers between devices, padded_2(): before = lax.ppermute(last, axis, up)  11.5 us
    ppermute x1, waiting for transfers between devices, padded_2(): after = lax.ppermute(initial, axis, down)  7.53 us
    unnamed x29, local copies, waits for them, and re-layouts  5.86 us
    dot_general x7, matrix products, correlate(): jnp.einsum('boc,bcxy->oxy', weights, stacked, preferred_element_type=jnp....  4.57 us
    another operation x7, local copies, waits for them, and re-layouts, correlate(): jnp.stack([window[:, :, col_shift:col_shift + width_cols] for col_shift i...  4.06 us
  transfers between devices with their start and end apart: 2, of which 2 were waited for; matrix products, arithmetic and copies ran while one was open for 0% of the time, Pallas kernels for 0%

profile of v1, /device:TPU:1, one launch (start us, length us, event | category | flops | bytes accessed | tf_op | source)
XLA Modules:
  0.0 71.5 jit_solution(2115531813992024407)
XLA Ops:
  0.0 11.5 %collective-permute-start = (bf16[64,3,128]{2,0,1:T(8,128)(2,1)}, bf16[64,3,128]{2,0,1:T(8,128)(2,1)S(1)}, u32[]{:S(2)}, u32[]{:S(2)}) collective-permute-start(bf16[64,3,128]{2,0,1:T(8,128)(2,1)} %param.2), channel_id=1, source_target_pairs={{0,8},{8,16},{16,24},{24,32},{32,40},{40,48},{48,56},{56,64},{64,7... | collective-permute-start | bytes 147464 | tf_op jit(solution)/shard_map/ppermute | solution.py:17
  11.5 1.3 %collective-permute-start.1 = (bf16[64,3,128]{2,0,1:T(8,128)(2,1)}, bf16[64,3,128]{2,0,1:T(8,128)(2,1)S(1)}, u32[]{:S(2)}, u32[]{:S(2)}) collective-permute-start(bf16[64,3,128]{2,0,1:T(8,128)(2,1)} %param.2), channel_id=1, source_target_pairs={{8,0},{16,8},{24,16},{32,24},{40,32},{48,40},{56,48},{64,56},{72,6... | collective-permute-start | bytes 147464 | tf_op jit(solution)/shard_map/ppermute | solution.py:18
  12.9 7.5 %collective-permute-done.1 = bf16[64,3,128]{2,0,1:T(8,128)(2,1)S(1)} collective-permute-done((bf16[64,3,128]{2,0,1:T(8,128)(2,1)}, bf16[64,3,128]{2,0,1:T(8,128)(2,1)S(1)}, u32[]{:S(2)}, u32[]{:S(2)}) %collective-permute-start.1) | collective-permute-done | bytes 49184 | tf_op jit(solution)/shard_map/ppermute | solution.py:18
  20.5 0.8 %pad_maximum_fusion = bf16[64,9,128]{2,0,1:T(8,128)(2,1)S(1)} fusion(bf16[64,3,128]{2,0,1:T(8,128)(2,1)S(1)} %collective-permute-done.1, bf16[64,3,128]{2,0,1:T(8,128)(2,1)} %param.2, bf16[64,3,128]{2,0,1:T(8,128)(2,1)S(1)} %collective-permute-done), kind=kLoop, calls=%fused_computation.170 | loop fusion | flops 147456 | bytes 294912 | tf_op jit(solution)/shard_map/concatenate | solution.py:19
  21.3 0.3 stack.179
  21.6 35.1 %all_to_all.5 = bf16[8,64,9,128]{3,1,2,0:T(8,128)(2,1)S(1)} all-to-all(bf16[8,64,9,128]{3,1,2,0:T(8,128)(2,1)S(1)} %stack.179), channel_id=1, replica_groups=mesh['space'=64,'chan'=8] {'chan'}, dimensions={0} | all-to-all | bytes 2359296 | tf_op jit(solution)/shard_map/all_to_all | solution.py:47
  57.1 0.2 fusion.38
  57.3 0.2 fusion.40
  57.6 0.2 fusion.42
  57.9 0.2 fusion.44
  58.1 0.8 %fusion.46 = (bf16[7,512,3,128]{3,1,2,0:T(8,128)(2,1)S(1)}, bf16[7,512,3,128]{3,1,2,0:T(8,128)(2,1)S(1)}, bf16[7,512,3,128]{3,1,2,0:T(8,128)(2,1)S(1)}, bf16[7,5...) fusion(bf16[7,512,3,128]{3,1,2,0:T(8,128)(2,1)S(1)} %fusion.44, ...), kind=kLoop, calls=%fused_computation.95 | loop fusion | bytes 3538944 | tf_op jit(solution)/shard_map/stack | solution.py:30
  58.9 0.2 fusion.50
  59.4 0.2 fusion.54
  59.9 1.0 %fusion.58 = (bf16[7,512,3,128]{3,1,2,0:T(8,128)(2,1)S(1)}, bf16[7,512,3,128]{3,1,2,0:T(8,128)(2,1)S(1)}, bf16[7,512,3,128]{3,1,2,0:T(8,128)(2,1)S(1)}, bf16[7,5...) fusion(bf16[7,512,3,128]{3,1,2,0:T(8,128)(2,1)S(1)} %fusion.56, bf16[512,9,128]{2,0,1:T(8,128)(2,1)S(1)} %bitcast.308, ...), kind=kLoop, calls=%fused_computation.107 | loop fusion | bytes 3145728 | tf_op jit(solution)/shard_map/stack | solution.py:30
  60.9 0.2 fusion.64
  61.2 0.2 fusion.66
  61.4 0.2 fusion.68
  61.6 0.8 %fusion.70 = (bf16[7,512,3,128]{3,1,2,0:T(8,128)(2,1)S(1)}, bf16[7,512,3,128]{3,1,2,0:T(8,128)(2,1)S(1)}, bf16[7,512,3,128]{3,1,2,0:T(8,128)(2,1)S(1)}, bf16[7,512,3,128]{3,1,2,0:T(8,128)(2,1)S(1)}) fusion(bf16[7,512,3,128]{3,1,2,0:T(8,128)(2,1)S(1)} %fusion.68, bf16[512,9,128]{2,0,1:T(8,128)(2,1)S(1)} %bitcast.313, ...), kind=kLoop, calls=%fused_computation.119 | loop fusion | bytes 2752512 | tf_op jit(solution)/shard_map/stack | solution.py:30
  62.7 0.4 fusion.80
  63.1 0.6 fusion.82
  63.7 0.2 fusion.92
  64.0 0.4 fusion.94
  64.4 0.2 fusion.106
  64.6 1.0 %copy-done = bf16[7,7,64,512]{3,2,1,0:T(8,128)(2,1)S(1)} copy-done((bf16[7,7,64,512]{3,2,1,0:T(8,128)(2,1)S(1)}, bf16[7,7,64,512]{3,2,1,0:T(8,128)(2,1)}, u32[]{:S(2)}) %copy-start) | copy-done | bytes 3211288
  65.6 0.6 convolution_bitcast_fusion
  66.2 0.6 convolution_bitcast_fusion.1
  66.8 0.6 convolution_bitcast_fusion.2
  67.3 0.6 convolution_bitcast_fusion.3
  67.9 0.6 convolution_bitcast_fusion.4
  68.5 0.2 fusion.26
  69.7 0.6 convolution_bitcast_fusion.5
  70.3 1.2 %fusion.8 = bf16[64,3,128]{2,0,1:T(8,128)(2,1)} fusion(f32[3,128,64]{1,2,0:T(8,128)S(1)} %convolution_bitcast_fusion, f32[3,128,64]{1,2,0:T(8,128)S(1)} %convolution_bitcast_fusion.1, f32[3,128,64]{1,2,0:T(8,128)S(1)} %convolution_bitcast_fusion.2, f32[3,128,64]{1,2,0:T(8,128)S(1)} %convolution_bitcast_fusion.3, ...), kind=kOutput, calls=%fused_computation.57 | convolution fusion | flops 176381952 | bytes 3899392 | tf_op jit(solution)/shard_map/boc,bcxy->oxy/dot_general | solution.py:34
  (19 shorter events, 2.5 us)
Async XLA Ops:
  0.0 12.9 %collective-permute-start = (bf16[64,3,128]{2,0,1:T(8,128)(2,1)}, bf16[64,3,128]{2,0,1:T(8,128)(2,1)S(1)}, u32[]{:S(2)}, u32[]{:S(2)}) collective-permute-start(bf16[64,3,128]{2,0,1:T(8,128)(2,1)} %param.2), channel_id=1, source_target_pairs={{0,8},{8,16},{16,24},{24,32},{32,40},{40,48},{48,56},{56,64},{64,7... | collective-permute-start | bytes 147464 | tf_op jit(solution)/shard_map/ppermute | solution.py:17
  11.5 9.0 %collective-permute-start.1 = (bf16[64,3,128]{2,0,1:T(8,128)(2,1)}, bf16[64,3,128]{2,0,1:T(8,128)(2,1)S(1)}, u32[]{:S(2)}, u32[]{:S(2)}) collective-permute-start(bf16[64,3,128]{2,0,1:T(8,128)(2,1)} %param.2), channel_id=1, source_target_pairs={{8,0},{16,8},{24,16},{32,24},{40,32},{48,40},{56,48},{64,56},{72,6... | collective-permute-start | bytes 147464 | tf_op jit(solution)/shard_map/ppermute | solution.py:18
  63.7 1.9 %copy-start = (bf16[7,7,64,512]{3,2,1,0:T(8,128)(2,1)S(1)}, bf16[7,7,64,512]{3,2,1,0:T(8,128)(2,1)}, u32[]{:S(2)}) copy-start(bf16[7,7,64,512]{3,2,1,0:T(8,128)(2,1)} %param.3) | copy-start | bytes 9633796
  69.5 0.8 %copy-start.1 = (bf16[64,3,128]{2,0,1:T(8,128)(2,1)S(1)}, bf16[64,3,128]{2,0,1:T(8,128)(2,1)}, u32[]{:S(2)}) copy-start(bf16[64,3,128]{2,0,1:T(8,128)(2,1)} %param.2) | copy-start | bytes 147460
